TPU v7x, 32 devices: a whole 2x2x4 slice. The times are simulated.
32 devices in a mesh: dp: 4 (over y, core), row: 2 (over x), col: 4 (over z).
Axes of the slice: x: 2, y: 2, z: 4, core: 2. Of those that a mesh axis runs over, the one named last changes fastest.
Arguments:
- inputs: bfloat16 [2048, 6144], P('dp', 'row'), may hold values from -600 to 600
- saved_qkv: bfloat16 [2048, 3, 3072], P('dp', None, 'col'), may hold values from -6 to 6
- saved_up: bfloat16 [2048, 12288], P('dp', 'col'), may hold values from -6 to 6
- cotangent: bfloat16 [2048, 6144], P('dp', 'row'), may hold values from -6 to 6
- weight_qkv: bfloat16 [6144, 3, 3072], P('row', None, 'col'), may hold values from -0.078125 to 0.078125
- weight_up: bfloat16 [6144, 12288], P('row', 'col'), may hold values from -0.078125 to 0.078125
- weight_attn: bfloat16 [3072, 6144], P('col', 'row'), may hold values from -0.109375 to 0.109375
- weight_down: bfloat16 [12288, 6144], P('col', 'row'), may hold values from -0.0546875 to 0.0546875
Outputs:
- grad_inputs: bfloat16 [2048, 6144], P(('dp', 'col'), 'row')
- grad_qkv: bfloat16 [2, 4, 768, 3, 3072], P('row', 'dp', None, None, 'col')
- grad_up: bfloat16 [2, 4, 768, 12288], P('row', 'dp', None, 'col')
- grad_attn: bfloat16 [4, 4, 192, 6144], P('col', 'dp', None, 'row')
- grad_down: bfloat16 [4, 4, 768, 6144], P('col', 'dp', None, 'row')
All inputs are finite; a program needn't handle non-finite values.
Results may differ from a plain program's by a relative error of at most 0.0039.
The roundings to bfloat16 on the way count: a program that leaves them out, or rounds other values in their place, can miss the bound.
Values may be sent and summed in bfloat16 or wider, within the bound.
No kernel may reach another device: no remote copies, remote signals or barrier semaphores. Data moves between devices by JAX's collectives and lax.ppermute only.
A program may use at most 192 MiB of HBM per device.

v0:
```python
import jax
import jax.numpy as jnp
from jax import lax
from jax.sharding import PartitionSpec as P

HD = 128
S = 256
EPS = 1e-06
SQRT_HALF = 0.7071067811865476
INV_ROOT_TWO_PI = 0.3989422804014327


def gelu_exact(values):
    return 0.5 * values * (1.0 + jax.scipy.special.erf(values * SQRT_HALF))


def gelu_slope(values):
    cumul = 0.5 * (1.0 + jax.scipy.special.erf(values * SQRT_HALF))
    return cumul + values * jnp.exp(-0.5 * values * values) * INV_ROOT_TWO_PI


def head_norm(values):
    average = jnp.mean(values, axis=-1, keepdims=True)
    centred = values - average
    inv_std = lax.rsqrt(jnp.mean(centred * centred, axis=-1, keepdims=True) + EPS)
    return (centred * inv_std, inv_std)


def head_norm_back(normed, inv_std, upstream):
    first = jnp.mean(upstream, axis=-1, keepdims=True)
    cross = jnp.mean(upstream * normed, axis=-1, keepdims=True)
    return inv_std * (upstream - first - normed * cross)


def body(inputs, saved_qkv, saved_up, cotangent, weight_qkv, weight_up, weight_attn, weight_down):
    f32 = jnp.float32
    bf16 = jnp.bfloat16
    tok_rows, feat_local = inputs.shape
    head_cols = saved_qkv.shape[2]
    up_cols = saved_up.shape[1]
    n_row = lax.axis_size("row")
    n_col = lax.axis_size("col")
    width = feat_local * n_row
    head_count = head_cols // HD
    images = tok_rows // S
    values = inputs.astype(f32)
    first_sum, square_sum = lax.psum(
        (jnp.sum(values, axis=1), jnp.sum(values * values, axis=1)), "row"
    )
    average = (first_sum / width)[:, None]
    inv_std = lax.rsqrt((square_sum / width)[:, None] - average * average + EPS)
    normed = (values - average) * inv_std
    normed_b = normed.astype(bf16)
    qkv5 = saved_qkv.reshape(images, S, 3, head_count, HD)
    query = qkv5[:, :, 0]
    keyed = qkv5[:, :, 1]
    valued = qkv5[:, :, 2]
    q_norm, q_inv = head_norm(query.astype(f32))
    k_norm, k_inv = head_norm(keyed.astype(f32))
    qn_b = q_norm.astype(bf16)
    kn_b = k_norm.astype(bf16)
    scale = HD ** (-0.5)
    scores = jnp.einsum("bqhd,bkhd->bhqk", qn_b, kn_b, preferred_element_type=f32) * scale
    expo = jnp.exp(scores)
    probs = expo / jnp.sum(expo, axis=-1, keepdims=True)
    probs_b = probs.astype(bf16)
    attended = jnp.einsum("bhqk,bkhd->bqhd", probs_b, valued, preferred_element_type=f32).astype(
        bf16
    )
    attended = attended.reshape(tok_rows, head_cols)
    hidden_b = gelu_exact(saved_up.astype(f32)).astype(bf16)
    part_attn = jnp.einsum("td,ad->ta", cotangent, weight_attn, preferred_element_type=f32)
    part_hidden = jnp.einsum("td,fd->tf", cotangent, weight_down, preferred_element_type=f32)
    sum_attn, sum_hidden = lax.psum((part_attn, part_hidden), "row")
    grad_o = sum_attn.astype(bf16)
    grad_pre = (sum_hidden * gelu_slope(saved_up.astype(f32))).astype(bf16)
    grad_o4 = grad_o.reshape(images, S, head_count, HD)
    grad_probs = jnp.einsum("bqhd,bkhd->bhqk", grad_o4, valued, preferred_element_type=f32)
    grad_value = jnp.einsum("bhqk,bqhd->bkhd", probs_b, grad_o4, preferred_element_type=f32).astype(
        bf16
    )
    rowdot = jnp.sum(probs * grad_probs, axis=-1, keepdims=True)
    grad_scores = (probs * (grad_probs - rowdot) * scale).astype(bf16)
    grad_qn = jnp.einsum("bhqk,bkhd->bqhd", grad_scores, kn_b, preferred_element_type=f32)
    grad_kn = jnp.einsum("bhqk,bqhd->bkhd", grad_scores, qn_b, preferred_element_type=f32)
    grad_query = head_norm_back(q_norm, q_inv, grad_qn).astype(bf16)
    grad_key = head_norm_back(k_norm, k_inv, grad_kn).astype(bf16)
    grad_flat = jnp.stack([grad_query, grad_key, grad_value], axis=2).reshape(
        tok_rows, 3 * head_cols
    )
    flat_weight = weight_qkv.reshape(feat_local, 3 * head_cols)
    share_rows = tok_rows // n_col
    total = jnp.einsum("ta,da->td", grad_flat, flat_weight, preferred_element_type=f32)
    grad_normed = lax.psum_scatter(
        total + jnp.einsum("tf,df->td", grad_pre, weight_up, preferred_element_type=f32),
        "col",
        scatter_dimension=0,
        tiled=True,
    )
    first_row = lax.axis_index("col") * share_rows
    normed_share = lax.dynamic_slice_in_dim(normed, first_row, share_rows, 0)
    inv_share = lax.dynamic_slice_in_dim(inv_std, first_row, share_rows, 0)
    cot_share = lax.dynamic_slice_in_dim(cotangent, first_row, share_rows, 0)
    sum_grad, sum_cross = lax.psum(
        (jnp.sum(grad_normed, axis=1), jnp.sum(grad_normed * normed_share, axis=1)), "row"
    )
    branch_term = (
        grad_normed - (sum_grad / width)[:, None] - normed_share * (sum_cross / width)[:, None]
    )
    grad_inputs = (cot_share.astype(f32) + inv_share * branch_term).astype(bf16)
    moved_normed, moved_attended, moved_hidden = (
        lax.all_to_all(normed_b, "dp", split_axis=1, concat_axis=0, tiled=True),
        lax.all_to_all(attended, "dp", split_axis=1, concat_axis=0, tiled=True),
        lax.all_to_all(hidden_b, "dp", split_axis=1, concat_axis=0, tiled=True),
    )
    cot_piece = lax.all_gather(cotangent, "dp", axis=0, tiled=True)
    flat_piece = lax.all_gather(grad_flat, "dp", axis=0, tiled=True)
    pre_piece = lax.all_gather(grad_pre, "dp", axis=0, tiled=True)
    new_qkv = jnp.einsum("td,ta->da", moved_normed, flat_piece, preferred_element_type=f32)
    new_up = jnp.einsum("td,tf->df", moved_normed, pre_piece, preferred_element_type=f32)
    new_attn = jnp.einsum("ta,td->ad", moved_attended, cot_piece, preferred_element_type=f32)
    new_down = jnp.einsum("tf,td->fd", moved_hidden, cot_piece, preferred_element_type=f32)
    grad_qkv = new_qkv.astype(bf16).reshape(1, 1, new_qkv.shape[0], 3, head_cols)
    grad_up = new_up.astype(bf16).reshape(1, 1, new_up.shape[0], up_cols)
    grad_attn = new_attn.astype(bf16).reshape(1, 1, new_attn.shape[0], feat_local)
    grad_down = new_down.astype(bf16).reshape(1, 1, new_down.shape[0], feat_local)
    return (grad_inputs, grad_qkv, grad_up, grad_attn, grad_down)


def solution(mesh):
    return jax.shard_map(
        body,
        mesh=mesh,
        in_specs=(
            P("dp", "row"),
            P("dp", None, "col"),
            P("dp", "col"),
            P("dp", "row"),
            P("row", None, "col"),
            P("row", "col"),
            P("col", "row"),
            P("col", "row"),
        ),
        out_specs=(
            P(("dp", "col"), "row"),
            P("row", "dp", None, None, "col"),
            P("row", "dp", None, "col"),
            P("col", "dp", None, "row"),
            P("col", "dp", None, "row"),
        ),
        check_vma=False,
    )
```

profile of v0, /device:TPU:0, one launch (start us, length us, event | category | flops | bytes accessed | tf_op | source)
XLA Modules:
  0.0 490.4 jit_solution(17388915969645549124)
XLA Ops:
  8.0 0.0 all-reduce.5.cloned.1.call-start
  8.0 16.4 %fusion.87 = f32[512,3072]{1,0:T(8,128)} fusion(bf16[512,3072]{1,0:T(8,128)(2,1)} %param.11, bf16[3072,3072]{1,0:T(8,128)(2,1)} %param.15), kind=kOutput, calls=%fused_computation.110 | convolution fusion | flops 9663676416 | bytes 28311552 | tf_op jit(solution)/shard_map/td,fd->tf/dot_general | solution.py:73
  24.5 0.0 all-gather.4.cloned.1.call-start
  24.5 7.2 %fusion.85 = f32[512,768]{1,0:T(8,128)} fusion(bf16[512,3072]{1,0:T(8,128)(2,1)} %param.11, bf16[768,3072]{1,0:T(8,128)(2,1)} %param.14), kind=kOutput, calls=%fused_computation.108 | convolution fusion | flops 2415919104 | bytes 9437184 | tf_op jit(solution)/shard_map/td,ad->ta/dot_general | solution.py:72
  31.7 1.0 convert_reduce_fusion
  32.7 79.4 %all-reduce.6 = (bf16[512,768]{1,0:T(8,128)(2,1)S(1)}, f32[512]{0:T(512)S(1)}, f32[512]{0:T(512)S(1)}) all-reduce(f32[512,768]{1,0:T(8,128)} %fusion.85, f32[512]{0:T(512)S(1)} %get-tuple-element.16, f32[512]{0:T(512)S(1)} %get-tuple-element.15), channel_id=1, replica_groups=mesh['dp'=4,'row'=2,'col'=4] {'row'}, use_global_device_ids=true, to_apply=%region_9.0 | all-reduce | flops 394240 | bytes 2367488 | tf_op jit(solution)/shard_map/psum | solution.py:74
  112.2 0.9 reshape.107
  113.1 0.6 copy.35
  113.7 2.8 copy.25
  116.5 2.1 reshape.99
  118.7 3.8 fusion.80
  122.4 2.5 copy.54
  124.9 0.2 convert_reduce_fusion.1
  125.1 0.2 fusion.47
  125.3 0.2 fusion.36
  125.6 2.2 fusion.55
  127.8 2.5 fusion.17
  130.4 7.8 %bitcast_reduce_fusion = (f32[2,256,6]{1,2,0:T(8,128)S(1)}, f32[2,256,6]{1,2,0:T(8,128)S(1)}, f32[2,6,128,256]{3,2,1,0:T(8,128)}) fusion(f32[2,256,6]{1,2,0:T(8,128)S(1)} %add_rsqrt_fusion, f32[2,256,6]{1,2,0:T(8,128)S(1)} %broadcast_multiply_fusion.4, bf16[2,256,1,6,128]{1,0,4,3,2:T(2,128)(2,1)S(1)} %get-tuple-element.34, f32[2,6,256,256]{2,3,1,0:T(8,128)} %fusion.55, ...), kind=kOutput, calls=%fused_computation.66 | convolution fusion | flops 212333824 | bytes 9523200 | tf_op jit(solution)/shard_map/bhqk,bqhd->bkhd/dot_general | solution.py:85
  138.2 7.7 %bitcast_reduce_fusion.1 = (f32[2,256,6]{1,2,0:T(8,128)S(1)}, f32[2,256,6]{1,2,0:T(8,128)S(1)}, f32[2,6,128,256]{3,2,1,0:T(8,128)}) fusion(f32[2,256,6]{1,2,0:T(8,128)S(1)} %add_rsqrt_fusion.1, f32[2,256,6]{1,2,0:T(8,128)S(1)} %broadcast_multiply_fusion.5, bf16[2,256,1,6,128]{1,0,4,3,2:T(2,128)(2,1)S(1)} %get-tuple-element.33, ...), kind=kOutput, calls=%fused_computation.68 | convolution fusion | flops 212333824 | bytes 9523200 | tf_op jit(solution)/shard_map/bhqk,bkhd->bqhd/dot_general | solution.py:84
  145.9 2.1 fusion.52
  148.1 0.1 copy-done.8
  148.2 0.4 fusion.53
  148.6 0.7 copy-done.10
  149.2 0.8 fusion.50
  150.0 0.3 pad_maximum_fusion
  150.3 2.4 copy.37
  152.7 1.9 copy.60
  154.6 0.0 all-gather.4.cloned.1.call-update
  154.6 0.0 reduce-scatter.2.cloned.1.call-start
  154.7 19.4 %copy.38 = bf16[3072,3,768]{0,2,1:T(8,128)(2,1)} copy(bf16[3072,3,768]{2,0,1:T(8,128)(2,1)} %param.12) | data formatting | bytes 28311552 | tf_op args[4]
  174.1 12.6 %fusion.86 = f32[512,3072]{1,0:T(8,128)} fusion(bf16[512,2304]{0,1:T(8,128)(2,1)S(1)} %bitcast.152, bf16[3072,2304]{0,1:T(8,128)(2,1)} %bitcast.147), kind=kOutput, calls=%fused_computation.109 | convolution fusion | flops 7247757312 | bytes 22806528 | tf_op jit(solution)/shard_map/ta,da->td/dot_general | solution.py:93
  186.7 27.9 %all-reduce.5.cloned.1.call-done = f32[512,3072]{1,0:T(8,128)} async-done(((f32[512,3072]{1,0:T(8,128)}), f32[512,3072]{1,0:T(8,128)}) %all-reduce.5.cloned.1.call-update) | async-done | bytes 6291472 | tf_op jit(solution)/shard_map/psum | solution.py:74
  214.6 7.8 %fusion.11 = (bf16[512,3072]{1,0:T(8,128)(2,1)}, bf16[512,3072]{1,0:T(8,128)(2,1)S(1)}) fusion(bf16[512,3072]{1,0:T(8,128)(2,1)} %param.10, f32[512,3072]{1,0:T(8,128)} %all-reduce.5.cloned.1.call-done), kind=kLoop, calls=%fused_computation.19 | loop fusion | flops 22020096 | bytes 15728640 | tf_op jit(solution)/shard_map/convert_element_type | solution.py:71
  222.4 17.5 %convolution_add_fusion = f32[512,3072]{1,0:T(8,128)} fusion(f32[512,3072]{1,0:T(8,128)} %fusion.86, bf16[512,3072]{1,0:T(8,128)(2,1)S(1)} %get-tuple-element.31, bf16[3072,3072]{1,0:T(8,128)(2,1)} %param.13), kind=kOutput, calls=%fused_computation.23 | convolution fusion | flops 9665249280 | bytes 34603008 | tf_op jit(solution)/shard_map/tf,df->td/dot_general | solution.py:95
  240.0 0.0 reduce-scatter.2.cloned.1.call-update
  240.0 0.0 all-gather.8.cloned.1.call-start
  240.1 0.5 all-gather.8.cloned.1.call-update
  240.6 0.0 all-gather.6.cloned.1.call-start
  240.6 0.5 all-gather.6.cloned.1.call-update
  241.2 3.6 fusion.51
  244.8 4.0 copy.42
  248.8 3.2 all_to_all.46
  252.0 4.7 all-to-all-start.1
  256.7 4.0 fusion.72
  260.7 1.9 copy.96
  262.6 14.6 %all-to-all-done.1 = bf16[512,4,192]{0,2,1:T(8,128)(2,1)} async-done(((bf16[512,4,192]{0,2,1:T(8,128)(2,1)}), bf16[512,4,192]{0,2,1:T(8,128)(2,1)}, u32[]{:S(2)}, u32[]{:S(2)}) %all-to-all-start.1) | async-done | bytes 786464 | tf_op jit(solution)/shard_map/all_to_all | solution.py:113
  277.2 4.9 %all-to-all-start = ((bf16[512,4,768]{2,0,1:T(8,128)(2,1)}), bf16[512,4,768]{2,0,1:T(8,128)(2,1)}, u32[]{:S(2)}, u32[]{:S(2)}) async-start(bf16[512,4,768]{2,0,1:T(8,128)(2,1)} %bitcast.146), calls=%async_computation.1 | async-start | bytes 6291456 | tf_op jit(solution)/shard_map/all_to_all | solution.py:112
  282.1 0.1 dynamic-slice.3
  282.2 2.1 copy.59
  284.3 1.9 copy.95
  286.2 67.0 %all-to-all-done = bf16[512,4,768]{2,0,1:T(8,128)(2,1)} async-done(((bf16[512,4,768]{2,0,1:T(8,128)(2,1)}), bf16[512,4,768]{2,0,1:T(8,128)(2,1)}, u32[]{:S(2)}, u32[]{:S(2)}) %all-to-all-start) | async-done | bytes 3145760 | tf_op jit(solution)/shard_map/all_to_all | solution.py:112
  353.2 4.7 all-to-all-start.2
  357.9 0.0 all-gather.4.cloned.1.call-done
  357.9 13.2 %convolution_convert_fusion.2 = bf16[768,2304]{1,0:T(8,128)(2,1)} fusion(bf16[2048,768]{1,0:T(8,128)(2,1)} %bitcast.11, bf16[2048,2304]{0,1:T(8,128)(2,1)} %all-gather.4.cloned.1.call-done), kind=kOutput, calls=%fused_computation.22 | convolution fusion | flops 7249526784 | bytes 16121856 | tf_op jit(solution)/shard_map/td,ta->da/dot_general | solution.py:119
  371.1 4.5 copy.40
  375.6 3.7 copy.45
  379.3 2.7 fusion.79
  382.1 5.1 %all-reduce = (f32[128]{0:T(128)S(1)}, f32[128]{0:T(128)S(1)}) all-reduce(f32[128]{0:T(128)S(1)} %get-tuple-element.18, f32[128]{0:T(128)S(1)} %get-tuple-element.17), channel_id=1, replica_groups=mesh['dp'=4,'row'=2,'col'=4] {'row'}, use_global_device_ids=true, to_apply=%region_20.0 | all-reduce | flops 256 | bytes 2048 | tf_op jit(solution)/shard_map/psum | solution.py:104
  387.2 3.2 add_convert_fusion
  390.4 8.2 %fusion.14 = bf16[1,1,192,3072]{3,2,1,0:T(8,128)(2,1)} fusion(bf16[2048,192]{0,1:T(8,128)(2,1)S(1)} %bitcast.154, bf16[2048,3072]{1,0:T(8,128)(2,1)} %all-gather.8.cloned.1.call-done), kind=kOutput, calls=%fused_computation.27 | convolution fusion | flops 2416508928 | bytes 14548992 | tf_op jit(solution)/shard_map/ta,td->ad/dot_general | solution.py:121
  398.6 11.4 %all-to-all-done.2 = bf16[512,4,768]{2,0,1:T(8,128)(2,1)} async-done(((bf16[512,4,768]{2,0,1:T(8,128)(2,1)}), bf16[512,4,768]{2,0,1:T(8,128)(2,1)}, u32[]{:S(2)}, u32[]{:S(2)}) %all-to-all-start.2) | async-done | bytes 3145760 | tf_op jit(solution)/shard_map/all_to_all | solution.py:114
  410.0 15.5 %fusion.13 = bf16[1,1,768,3072]{3,2,1,0:T(8,128)(2,1)} fusion(bf16[2048,768]{1,0:T(8,128)(2,1)} %bitcast.19, bf16[2048,3072]{1,0:T(8,128)(2,1)} %all-gather.8.cloned.1.call-done), kind=kOutput, calls=%fused_computation.25 | convolution fusion | flops 9666035712 | bytes 20447232 | tf_op jit(solution)/shard_map/tf,td->fd/dot_general | solution.py:122
  425.5 41.8 %all-gather.6.cloned.1.call-done = bf16[2048,3072]{1,0:T(8,128)(2,1)} async-done(((bf16[512,3072]{1,0:T(8,128)(2,1)}), bf16[2048,3072]{1,0:T(8,128)(2,1)}) %all-gather.6.cloned.1.call-update) | async-done | bytes 12582928 | tf_op jit(solution)/shard_map/all_gather | solution.py:118
  467.3 15.3 %fusion.12 = bf16[1,1,768,3072]{3,2,1,0:T(8,128)(2,1)} fusion(bf16[2048,768]{1,0:T(8,128)(2,1)} %bitcast.11, bf16[2048,3072]{1,0:T(8,128)(2,1)} %all-gather.6.cloned.1.call-done), kind=kOutput, calls=%fused_computation.24 | convolution fusion | flops 9666035712 | bytes 20447232 | tf_op jit(solution)/shard_map/td,tf->df/dot_general | solution.py:120
  (34 shorter events, 0.1 us)
Async XLA Ops:
  8.0 206.6 %all-reduce.5.cloned.1.call-start = ((), (), s32[]{:S(2)}) async-start(), calls=%async_computation.4 | async-start | bytes 12582912 | tf_op jit(solution)/shard_map/psum | solution.py:74
  24.4 7.3 %copy-start = (bf16[512,3072]{1,0:T(8,128)(2,1)S(1)}, bf16[512,3072]{1,0:T(8,128)(2,1)}, u32[]{:S(2)}) copy-start(bf16[512,3072]{1,0:T(8,128)(2,1)} %param.8) | copy-start | bytes 9437188
  24.5 333.5 %all-gather.4.cloned.1.call-start = ((), (), s32[]{:S(2)}) async-start(), calls=%async_computation.6 | async-start | bytes 11796480 | tf_op jit(solution)/shard_map/all_gather | solution.py:117
  124.9 2.9 copy-start.6
  145.9 2.2 copy-start.8
  145.9 3.3 copy-start.10
  154.6 19.5 %copy-start.4 = (bf16[288,8,2,256]{3,1,2,0:T(8,128)(2,1)S(1)}, bf16[288,8,2,256]{3,1,2,0:T(8,128)(2,1)}, u32[]{:S(2)}) copy-start(bf16[288,8,2,256]{3,1,2,0:T(8,128)(2,1)} %copy.60) | copy-start | bytes 7077892
  154.6 224.7 %reduce-scatter.2.cloned.1.call-start = ((), (), s32[]{:S(2)}) async-start(), calls=%async_computation.5 | async-start | bytes 7864320 | tf_op jit(solution)/shard_map/reduce_scatter | solution.py:94
  222.4 17.5 %copy-start.2 = (bf16[512,3072]{1,0:T(8,128)(2,1)}, bf16[512,3072]{1,0:T(8,128)(2,1)S(1)}, u32[]{:S(2)}) copy-start(bf16[512,3072]{1,0:T(8,128)(2,1)S(1)} %get-tuple-element.31) | copy-start | bytes 9437188
  240.0 1.2 copy-start.7
  240.0 150.4 %all-gather.8.cloned.1.call-start = ((), (), s32[]{:S(2)}) async-start(), calls=%async_computation.8 | async-start | bytes 15728640 | tf_op jit(solution)/shard_map/all_gather | solution.py:116
  240.6 226.7 %all-gather.6.cloned.1.call-start = ((), (), s32[]{:S(2)}) async-start(), calls=%async_computation.7 | async-start | bytes 15728640 | tf_op jit(solution)/shard_map/all_gather | solution.py:118
  244.8 11.9 %copy-start.1 = (bf16[512,3072]{1,0:T(8,128)(2,1)S(1)}, bf16[512,3072]{1,0:T(8,128)(2,1)}, u32[]{:S(2)}) copy-start(bf16[512,3072]{1,0:T(8,128)(2,1)} %param.8) | copy-start | bytes 9437188
  252.0 25.2 %all-to-all-start.1 = ((bf16[512,4,192]{0,2,1:T(8,128)(2,1)}), bf16[512,4,192]{0,2,1:T(8,128)(2,1)}, u32[]{:S(2)}, u32[]{:S(2)}) async-start(bf16[512,4,192]{0,2,1:T(8,128)(2,1)} %all_to_all.46), calls=%async_computation.2 | async-start | bytes 1572864 | tf_op jit(solution)/shard_map/all_to_all | solution.py:113
  277.2 7.1 %copy-start.3 = (bf16[512,3072]{1,0:T(8,128)(2,1)S(1)}, bf16[512,3072]{1,0:T(8,128)(2,1)}, u32[]{:S(2)}) copy-start(bf16[512,3072]{1,0:T(8,128)(2,1)} %get-tuple-element.30) | copy-start | bytes 9437188
  277.2 76.0 %all-to-all-start = ((bf16[512,4,768]{2,0,1:T(8,128)(2,1)}), bf16[512,4,768]{2,0,1:T(8,128)(2,1)}, u32[]{:S(2)}, u32[]{:S(2)}) async-start(bf16[512,4,768]{2,0,1:T(8,128)(2,1)} %bitcast.146), calls=%async_computation.1 | async-start | bytes 6291456 | tf_op jit(solution)/shard_map/all_to_all | solution.py:112
  353.2 56.7 %all-to-all-start.2 = ((bf16[512,4,768]{2,0,1:T(8,128)(2,1)}), bf16[512,4,768]{2,0,1:T(8,128)(2,1)}, u32[]{:S(2)}, u32[]{:S(2)}) async-start(bf16[512,4,768]{2,0,1:T(8,128)(2,1)} %bitcast.145), calls=%async_computation.3 | async-start | bytes 6291456 | tf_op jit(solution)/shard_map/all_to_all | solution.py:114
  379.3 7.8 %copy-start.5 = (f32[128,3072]{1,0:T(8,128)S(1)}, f32[128,3072]{1,0:T(8,128)}, u32[]{:S(2)}) copy-start(f32[128,3072]{1,0:T(8,128)} %reduce-scatter.2.cloned.1.call-done) | copy-start | bytes 4718596
  382.1 8.3 %copy-start.9 = (bf16[4,24,8,512]{3,2,0,1:T(8,128)(2,1)S(1)}, bf16[4,24,8,512]{3,2,0,1:T(8,128)(2,1)}, u32[]{:S(2)}) copy-start(bf16[4,24,8,512]{3,2,0,1:T(8,128)(2,1)} %copy.59) | copy-start | bytes 2359300
Sparse Core Ops, SparseCore 0:
  24.6 190.0 all-reduce.4
  240.1 110.7 reduce-scatter.1
Sparse Core Ops, SparseCore 1:
  154.7 64.6 all-gather.3
  242.0 127.3 all-gather.7
  371.4 95.8 all-gather.5
where the time goes:
time: 499 us; the launch traced here: 490 us
  waiting for transfers between devices  164 us (33%)
  matrix products  131 us (26%)
  blocking collectives  84.5 us (17%)
  local copies, waits for them, and re-layouts  58.4 us (12%)
  other arithmetic  22.3 us (4%)
  between operations  16.1 us (3%)
  starting transfers between devices  14.5 us (3%)
    psum x1, blocking collectives, body(): sum_attn, sum_hidden = lax.psum((part_attn, part_hidden), 'row')  79.4 us
    all_to_all x1, waiting for transfers between devices, body(): lax.all_to_all(normed_b, 'dp', split_axis=1, concat_axis=0, tiled=True)  67 us
    all_gather x1, waiting for transfers between devices, body(): pre_piece = lax.all_gather(grad_pre, 'dp', axis=0, tiled=True)  41.8 us
    unnamed x27, local copies, waits for them, and re-layouts  31 us
    psum x1, waiting for transfers between devices, body(): sum_attn, sum_hidden = lax.psum((part_attn, part_hidden), 'row')  27.9 us
    dot_general x1, matrix products, body(): jnp.einsum('tf,df->td', grad_pre, weight_up, preferred_element_type=f32)  17.5 us
    dot_general x1, matrix products, body(): jnp.einsum('td,fd->tf', cotangent, weight_down, preferred_element_type=f32)  16.4 us
    dot_general x1, matrix products, body(): jnp.einsum('tf,td->fd', moved_hidden, cot_piece, preferred_element_type=f32)  15.5 us
  transfers between devices with their start and end apart: 8, of which 5 were waited for; matrix products, arithmetic and copies ran while one was open for 36% of the time, Pallas kernels for 0%

commit v1 on v0

--- a/solution.py
+++ b/solution.py
@@ -8,6 +8,26 @@
 EPS = 1e-06
 SQRT_HALF = 0.7071067811865476
 INV_ROOT_TWO_PI = 0.3989422804014327
+
+
+def fix_gates_now(matrix, along_dim, array_here):
+    w2 = lax.axis_size("dp")
+    block_next = lax.axis_index("dp")
+    high, local_part, local_next = (w2, block_next, matrix.shape[along_dim])
+    items = [(i0, (i0 + 1) % high) for i0 in range(high)]
+    lanes = [(i0, (i0 - 1) % high) for i0 in range(high)]
+    clean = high // 2
+    y1 = y_new = matrix
+    block_now = array_here(matrix, local_part * local_next)
+    for nth in range(1, clean + 1):
+        y1 = lax.ppermute(y1, "dp", items)
+        if nth < high - clean:
+            y_new = lax.ppermute(y_new, "dp", lanes)
+            placed = array_here(y_new, (local_part + nth) % high * local_next)
+            block_now = block_now + placed
+        e_now = array_here(y1, (local_part - nth) % high * local_next)
+        block_now = block_now + e_now
+    return block_now
 
 
 def gelu_exact(values):
@@ -115,9 +135,17 @@
     )
     cot_piece = lax.all_gather(cotangent, "dp", axis=0, tiled=True)
     flat_piece = lax.all_gather(grad_flat, "dp", axis=0, tiled=True)
-    pre_piece = lax.all_gather(grad_pre, "dp", axis=0, tiled=True)
     new_qkv = jnp.einsum("td,ta->da", moved_normed, flat_piece, preferred_element_type=f32)
-    new_up = jnp.einsum("td,tf->df", moved_normed, pre_piece, preferred_element_type=f32)
+    new_up = fix_gates_now(
+        grad_pre,
+        0,
+        lambda part, offset: jnp.einsum(
+            "td,tf->df",
+            lax.dynamic_slice_in_dim(moved_normed, offset, part.shape[0], axis=0),
+            part,
+            preferred_element_type=f32,
+        ),
+    )
     new_attn = jnp.einsum("ta,td->ad", moved_attended, cot_piece, preferred_element_type=f32)
     new_down = jnp.einsum("tf,td->fd", moved_hidden, cot_piece, preferred_element_type=f32)
     grad_qkv = new_qkv.astype(bf16).reshape(1, 1, new_qkv.shape[0], 3, head_cols)

time: 499 us -> 551 us (1.10)
  matrix products: 131 us -> 157 us
  waiting for transfers between devices: 164 us -> 179 us
  starting transfers between devices: 14.5 us -> 24.1 us
    all_to_all x1, waiting for transfers between devices: 14.6 us -> 71.6 us  [body(): lax.all_to_all(attended, 'dp', split_axis=1, concat_axis=0, tiled=True)]
    ppermute x0 -> x3, waiting for transfers between devices: none -> 45.2 us  [the longest x1 45.1 us: fix_gates_now(): y_new = lax.ppermute(y_new, 'dp', lanes)]
    all_gather x1 -> x0, waiting for transfers between devices: 41.8 us -> none  [body(): pre_piece = lax.all_gather(grad_pre, 'dp', axis=0, tiled=True)]
    all_to_all x1, waiting for transfers between devices: 67 us -> 34.2 us  [body(): lax.all_to_all(normed_b, 'dp', split_axis=1, concat_axis=0, tiled=True)]
    dot_general x1 -> x4, matrix products: 15.3 us -> 41 us  [body(): jnp.einsum('td,tf->df', lax.dynamic_slice_in_dim(moved_normed, offset, pa...]
    all_to_all x1, waiting for transfers between devices: 11.4 us -> 0.01 us  [body(): lax.all_to_all(hidden_b, 'dp', split_axis=1, concat_axis=0, tiled=True)]
    all_to_all x1, starting transfers between devices: 4.93 us -> 11.4 us  [body(): lax.all_to_all(normed_b, 'dp', split_axis=1, concat_axis=0, tiled=True)]
    unnamed x27 -> x25, local copies, waits for them, and re-layouts: 31 us -> 31.5 us
  transfers between devices with their start and end apart: 8 -> 10, of which waited for: 5 -> 4; matrix products, arithmetic and copies ran while one was open for 36% -> 37% of each run, Pallas kernels for 0% -> 0%
where the time goes in v1:
time: 551 us; the launch traced here: 542 us
  waiting for transfers between devices  179 us (32%)
  matrix products  157 us (28%)
  blocking collectives  84.4 us (15%)
  local copies, waits for them, and re-layouts  58.9 us (11%)
  starting transfers between devices  24.1 us (4%)
  other arithmetic  22.6 us (4%)
  between operations  16.2 us (3%)
    psum x1, blocking collectives, body(): sum_attn, sum_hidden = lax.psum((part_attn, part_hidden), 'row')  79.4 us
    all_to_all x1, waiting for transfers between devices, body(): lax.all_to_all(attended, 'dp', split_axis=1, concat_axis=0, tiled=True)  71.6 us
    ppermute x1, waiting for transfers between devices, fix_gates_now(): y_new = lax.ppermute(y_new, 'dp', lanes)  45.1 us
    dot_general x4, matrix products, body(): jnp.einsum('td,tf->df', lax.dynamic_slice_in_dim(moved_normed, offset, pa...  41 us
    all_to_all x1, waiting for transfers between devices, body(): lax.all_to_all(normed_b, 'dp', split_axis=1, concat_axis=0, tiled=True)  34.2 us
    unnamed x25, local copies, waits for them, and re-layouts  31.5 us
    psum x1, waiting for transfers between devices, body(): sum_attn, sum_hidden = lax.psum((part_attn, part_hidden), 'row')  27.8 us
    dot_general x1, matrix products, body(): jnp.einsum('tf,df->td', grad_pre, weight_up, preferred_element_type=f32)  17.3 us
  transfers between devices with their start and end apart: 10, of which 4 were waited for; matrix products, arithmetic and copies ran while one was open for 37% of the time, Pallas kernels for 0%

profile of v1, /device:TPU:0, one launch (start us, length us, event | category | flops | bytes accessed | tf_op | source)
XLA Modules:
  0.0 542.1 jit_solution(18093880154042535752)
XLA Ops:
  8.0 0.0 all-reduce.5.cloned.1.call-start
  8.0 16.4 %fusion.98 = f32[512,3072]{1,0:T(8,128)} fusion(bf16[512,3072]{1,0:T(8,128)(2,1)} %param.11, bf16[3072,3072]{1,0:T(8,128)(2,1)} %param.15), kind=kOutput, calls=%fused_computation.121 | convolution fusion | flops 9663676416 | bytes 28311552 | tf_op jit(solution)/shard_map/td,fd->tf/dot_general | solution.py:93
  24.5 0.0 all-gather.3.cloned.1.call-start
  24.5 7.2 %fusion.96 = f32[512,768]{1,0:T(8,128)} fusion(bf16[512,3072]{1,0:T(8,128)(2,1)} %param.11, bf16[768,3072]{1,0:T(8,128)(2,1)} %param.14), kind=kOutput, calls=%fused_computation.119 | convolution fusion | flops 2415919104 | bytes 9437184 | tf_op jit(solution)/shard_map/td,ad->ta/dot_general | solution.py:92
  31.7 1.0 convert_reduce_fusion
  32.7 79.4 %all-reduce.6 = (bf16[512,768]{1,0:T(8,128)(2,1)S(1)}, f32[512]{0:T(512)S(1)}, f32[512]{0:T(512)S(1)}) all-reduce(f32[512,768]{1,0:T(8,128)} %fusion.96, f32[512]{0:T(512)S(1)} %get-tuple-element.16, f32[512]{0:T(512)S(1)} %get-tuple-element.15), channel_id=1, replica_groups=mesh['dp'=4,'row'=2,'col'=4] {'row'}, use_global_device_ids=true, to_apply=%region_9.0 | all-reduce | flops 394240 | bytes 2367488 | tf_op jit(solution)/shard_map/psum | solution.py:94
  112.2 0.9 reshape.107
  113.1 0.6 copy.35
  113.7 2.8 copy.25
  116.5 2.1 reshape.99
  118.7 3.8 fusion.91
  122.4 2.5 copy.54
  125.0 0.2 convert_reduce_fusion.1
  125.1 0.2 fusion.47
  125.4 0.2 fusion.36
  125.6 2.2 fusion.55
  127.9 2.5 fusion.17
  130.4 7.8 %bitcast_reduce_fusion = (f32[2,256,6]{1,2,0:T(8,128)S(1)}, f32[2,256,6]{1,2,0:T(8,128)S(1)}, f32[2,6,128,256]{3,2,1,0:T(8,128)}) fusion(f32[2,256,6]{1,2,0:T(8,128)S(1)} %add_rsqrt_fusion, f32[2,256,6]{1,2,0:T(8,128)S(1)} %broadcast_multiply_fusion.4, bf16[2,256,1,6,128]{1,0,4,3,2:T(2,128)(2,1)S(1)} %get-tuple-element.34, f32[2,6,256,256]{2,3,1,0:T(8,128)} %fusion.55, ...), kind=kOutput, calls=%fused_computation.66 | convolution fusion | flops 212333824 | bytes 9523200 | tf_op jit(solution)/shard_map/bhqk,bqhd->bkhd/dot_general | solution.py:105
  138.3 7.7 %bitcast_reduce_fusion.1 = (f32[2,256,6]{1,2,0:T(8,128)S(1)}, f32[2,256,6]{1,2,0:T(8,128)S(1)}, f32[2,6,128,256]{3,2,1,0:T(8,128)}) fusion(f32[2,256,6]{1,2,0:T(8,128)S(1)} %add_rsqrt_fusion.1, f32[2,256,6]{1,2,0:T(8,128)S(1)} %broadcast_multiply_fusion.5, bf16[2,256,1,6,128]{1,0,4,3,2:T(2,128)(2,1)S(1)} %get-tuple-element.33, ...), kind=kOutput, calls=%fused_computation.68 | convolution fusion | flops 212333824 | bytes 9523200 | tf_op jit(solution)/shard_map/bhqk,bkhd->bqhd/dot_general | solution.py:104
  146.0 2.2 fusion.52
  148.2 0.0 copy-done.7
  148.2 0.4 fusion.53
  148.6 0.6 copy-done.9
  149.3 0.8 fusion.50
  150.0 0.3 pad_maximum_fusion
  150.3 2.4 copy.37
  152.8 1.9 copy.60
  154.7 0.0 reduce-scatter.2.cloned.1.call-start
  154.7 19.4 %copy.38 = bf16[3072,3,768]{0,2,1:T(8,128)(2,1)} copy(bf16[3072,3,768]{2,0,1:T(8,128)(2,1)} %param.12) | data formatting | bytes 28311552 | tf_op args[4]
  174.1 12.7 %fusion.97 = f32[512,3072]{1,0:T(8,128)} fusion(bf16[512,2304]{0,1:T(8,128)(2,1)S(1)} %bitcast.154, bf16[3072,2304]{0,1:T(8,128)(2,1)} %bitcast.149), kind=kOutput, calls=%fused_computation.120 | convolution fusion | flops 7247757312 | bytes 22806528 | tf_op jit(solution)/shard_map/ta,da->td/dot_general | solution.py:113
  186.8 27.8 %all-reduce.5.cloned.1.call-done = f32[512,3072]{1,0:T(8,128)} async-done(((f32[512,3072]{1,0:T(8,128)}), f32[512,3072]{1,0:T(8,128)}) %all-reduce.5.cloned.1.call-update) | async-done | bytes 6291472 | tf_op jit(solution)/shard_map/psum | solution.py:94
  214.6 8.9 %fusion.11 = (bf16[512,3072]{1,0:T(8,128)(2,1)}, bf16[512,3072]{1,0:T(8,128)(2,1)}) fusion(bf16[512,3072]{1,0:T(8,128)(2,1)} %param.10, f32[512,3072]{1,0:T(8,128)} %all-reduce.5.cloned.1.call-done), kind=kLoop, calls=%fused_computation.20 | loop fusion | flops 22020096 | bytes 15728640 | tf_op jit(solution)/shard_map/convert_element_type | solution.py:91
  223.5 17.3 %convolution_add_fusion = f32[512,3072]{1,0:T(8,128)} fusion(f32[512,3072]{1,0:T(8,128)} %fusion.97, bf16[512,3072]{1,0:T(8,128)(2,1)} %get-tuple-element.31, bf16[3072,3072]{1,0:T(8,128)(2,1)} %param.13), kind=kOutput, calls=%fused_computation.23 | convolution fusion | flops 9665249280 | bytes 34603008 | tf_op jit(solution)/shard_map/tf,df->td/dot_general | solution.py:115
  240.9 0.0 all-gather.5.cloned.1.call-start
  240.9 0.5 all-gather.5.cloned.1.call-update
  241.4 0.1 collective-permute-start.1
  241.5 0.5 copy-done.6
  242.0 3.6 fusion.51
  245.6 3.9 copy.42
  249.5 3.2 all_to_all.46
  252.7 4.5 all-to-all-start.1
  257.2 4.0 fusion.83
  261.2 1.9 copy.96
  263.1 71.6 %all-to-all-done.1 = bf16[512,4,192]{0,2,1:T(8,128)(2,1)} async-done(((bf16[512,4,192]{0,2,1:T(8,128)(2,1)}), bf16[512,4,192]{0,2,1:T(8,128)(2,1)}, u32[]{:S(2)}, u32[]{:S(2)}) %all-to-all-start.1) | async-done | bytes 786464 | tf_op jit(solution)/shard_map/all_to_all | solution.py:133
  334.6 11.4 %all-to-all-start = ((bf16[512,4,768]{2,0,1:T(8,128)(2,1)}), bf16[512,4,768]{2,0,1:T(8,128)(2,1)}, u32[]{:S(2)}, u32[]{:S(2)}) async-start(bf16[512,4,768]{2,0,1:T(8,128)(2,1)} %bitcast.148), calls=%async_computation.1 | async-start | bytes 6291456 | tf_op jit(solution)/shard_map/all_to_all | solution.py:132
  346.0 3.4 collective-permute-start
  349.5 0.1 dynamic-slice.3
  349.5 2.1 copy.59
  351.6 1.9 copy.95
  353.5 34.2 %all-to-all-done = bf16[512,4,768]{2,0,1:T(8,128)(2,1)} async-done(((bf16[512,4,768]{2,0,1:T(8,128)(2,1)}), bf16[512,4,768]{2,0,1:T(8,128)(2,1)}, u32[]{:S(2)}, u32[]{:S(2)}) %all-to-all-start) | async-done | bytes 3145760 | tf_op jit(solution)/shard_map/all_to_all | solution.py:132
  387.8 4.7 all-to-all-start.2
  392.4 8.4 %fusion.62 = f32[768,3072]{1,0:T(8,128)} fusion(bf16[512,3072]{1,0:T(8,128)(2,1)} %get-tuple-element.31, bf16[2048,768]{1,0:T(8,128)(2,1)} %bitcast.11, s32[]{:T(128)S(6)} %select_n.33), kind=kOutput, calls=%fused_computation.87 | convolution fusion | flops 2415919104 | bytes 13369348 | tf_op jit(solution)/shard_map/td,tf->df/dot_general | solution.py:142
  400.8 8.4 %fusion.58 = f32[768,3072]{1,0:T(8,128)} fusion(bf16[512,3072]{1,0:T(8,128)(2,1)} %collective-permute-done.1, bf16[2048,768]{1,0:T(8,128)(2,1)} %bitcast.11, s32[]{:T(128)S(6)} %select_n.37), kind=kOutput, calls=%fused_computation.83 | convolution fusion | flops 2415919104 | bytes 13369348 | tf_op jit(solution)/shard_map/td,tf->df/dot_general | solution.py:142
  409.1 45.1 %collective-permute-done = bf16[512,3072]{1,0:T(8,128)(2,1)} collective-permute-done((bf16[512,3072]{1,0:T(8,128)(2,1)}, bf16[512,3072]{1,0:T(8,128)(2,1)}, u32[]{:S(2)}, u32[]{:S(2)}) %collective-permute-start) | collective-permute-done | bytes 3145760 | tf_op jit(solution)/shard_map/ppermute | solution.py:25
  454.3 8.4 %fusion.60 = f32[768,3072]{1,0:T(8,128)} fusion(bf16[512,3072]{1,0:T(8,128)(2,1)} %collective-permute-done, bf16[2048,768]{1,0:T(8,128)(2,1)} %bitcast.11, s32[]{:T(128)S(6)} %select_n.35), kind=kOutput, calls=%fused_computation.85 | convolution fusion | flops 2415919104 | bytes 13369348 | tf_op jit(solution)/shard_map/td,tf->df/dot_general | solution.py:142
  462.7 15.9 %fusion.13 = bf16[1,1,768,3072]{3,2,1,0:T(8,128)(2,1)} fusion(bf16[512,3072]{1,0:T(8,128)(2,1)} %collective-permute-done.2, f32[768,3072]{1,0:T(8,128)} %fusion.58, f32[768,3072]{1,0:T(8,128)} %fusion.62, f32[768,3072]{1,0:T(8,128)} %fusion.60, bf16[2048,768]{1,0:T(8,128)(2,1)} %bitcast.11, s32[]{:T(128)S(6)} %select_n.39), kind=kOutput, calls=%fused_computation.25 | convolution fusion | flops 2425356288 | bytes 36962308 | tf_op jit(solution)/shard_map/td,tf->df/dot_general | solution.py:142
  478.6 13.4 %convolution_convert_fusion.1 = bf16[768,2304]{1,0:T(8,128)(2,1)} fusion(bf16[2048,768]{1,0:T(8,128)(2,1)} %bitcast.11, bf16[2048,2304]{0,1:T(8,128)(2,1)} %all-gather.3.cloned.1.call-done), kind=kOutput, calls=%fused_computation.22 | convolution fusion | flops 7249526784 | bytes 16121856 | tf_op jit(solution)/shard_map/td,ta->da/dot_general | solution.py:138
  491.9 4.5 copy.40
  496.5 3.7 copy.45
  500.1 2.2 fusion.90
  502.3 5.0 all-reduce
  507.3 8.2 %fusion.14 = bf16[1,1,192,3072]{3,2,1,0:T(8,128)(2,1)} fusion(bf16[2048,192]{0,1:T(8,128)(2,1)S(1)} %bitcast.156, bf16[2048,3072]{1,0:T(8,128)(2,1)} %all-gather.5.cloned.1.call-done), kind=kOutput, calls=%fused_computation.27 | convolution fusion | flops 2416508928 | bytes 14548992 | tf_op jit(solution)/shard_map/ta,td->ad/dot_general | solution.py:149
  515.5 15.7 %fusion.12 = bf16[1,1,768,3072]{3,2,1,0:T(8,128)(2,1)} fusion(bf16[2048,768]{1,0:T(8,128)(2,1)} %bitcast.19, bf16[2048,3072]{1,0:T(8,128)(2,1)} %all-gather.5.cloned.1.call-done), kind=kOutput, calls=%fused_computation.24 | convolution fusion | flops 9666035712 | bytes 20447232 | tf_op jit(solution)/shard_map/tf,td->fd/dot_general | solution.py:150
  531.2 3.0 add_convert_fusion.1
  (38 shorter events, 0.2 us)
Async XLA Ops:
  8.0 206.6 %all-reduce.5.cloned.1.call-start = ((), (), s32[]{:S(2)}) async-start(), calls=%async_computation.4 | async-start | bytes 12582912 | tf_op jit(solution)/shard_map/psum | solution.py:94
  24.4 7.3 %copy-start = (bf16[512,3072]{1,0:T(8,128)(2,1)S(1)}, bf16[512,3072]{1,0:T(8,128)(2,1)}, u32[]{:S(2)}) copy-start(bf16[512,3072]{1,0:T(8,128)(2,1)} %param.8) | copy-start | bytes 9437188
  24.5 454.1 %all-gather.3.cloned.1.call-start = ((), (), s32[]{:S(2)}) async-start(), calls=%async_computation.6 | async-start | bytes 11796480 | tf_op jit(solution)/shard_map/all_gather | solution.py:137
  124.9 2.9 copy-start.5
  146.0 2.2 copy-start.7
  146.0 3.3 copy-start.9
  154.7 19.5 %copy-start.3 = (bf16[288,8,2,256]{3,1,2,0:T(8,128)(2,1)S(1)}, bf16[288,8,2,256]{3,1,2,0:T(8,128)(2,1)}, u32[]{:S(2)}) copy-start(bf16[288,8,2,256]{3,1,2,0:T(8,128)(2,1)} %copy.60) | copy-start | bytes 7077892
  154.7 345.5 %reduce-scatter.2.cloned.1.call-start = ((), (), s32[]{:S(2)}) async-start(), calls=%async_computation.5 | async-start | bytes 7864320 | tf_op jit(solution)/shard_map/reduce_scatter | solution.py:114
  240.8 1.1 copy-start.6
  240.9 266.5 %all-gather.5.cloned.1.call-start = ((), (), s32[]{:S(2)}) async-start(), calls=%async_computation.7 | async-start | bytes 15728640 | tf_op jit(solution)/shard_map/all_gather | solution.py:136
  241.4 108.0 %collective-permute-start.1 = (bf16[512,3072]{1,0:T(8,128)(2,1)}, bf16[512,3072]{1,0:T(8,128)(2,1)}, u32[]{:S(2)}, u32[]{:S(2)}) collective-permute-start(bf16[512,3072]{1,0:T(8,128)(2,1)} %get-tuple-element.31), channel_id=1, source_target_pairs={{0,8},{8,16},{16,24},{24,0},{1,9},{9,17},{17,25},{25,1},{2,10},{10... | collective-permute-start | bytes 9437192 | tf_op jit(solution)/shard_map/ppermute | solution.py:23
  245.6 11.6 %copy-start.1 = (bf16[512,3072]{1,0:T(8,128)(2,1)S(1)}, bf16[512,3072]{1,0:T(8,128)(2,1)}, u32[]{:S(2)}) copy-start(bf16[512,3072]{1,0:T(8,128)(2,1)} %param.8) | copy-start | bytes 9437188
  252.7 81.9 %all-to-all-start.1 = ((bf16[512,4,192]{0,2,1:T(8,128)(2,1)}), bf16[512,4,192]{0,2,1:T(8,128)(2,1)}, u32[]{:S(2)}, u32[]{:S(2)}) async-start(bf16[512,4,192]{0,2,1:T(8,128)(2,1)} %all_to_all.46), calls=%async_computation.2 | async-start | bytes 1572864 | tf_op jit(solution)/shard_map/all_to_all | solution.py:133
  334.6 17.0 %copy-start.2 = (bf16[512,3072]{1,0:T(8,128)(2,1)S(1)}, bf16[512,3072]{1,0:T(8,128)(2,1)}, u32[]{:S(2)}) copy-start(bf16[512,3072]{1,0:T(8,128)(2,1)} %get-tuple-element.30) | copy-start | bytes 9437188
  334.6 53.1 %all-to-all-start = ((bf16[512,4,768]{2,0,1:T(8,128)(2,1)}), bf16[512,4,768]{2,0,1:T(8,128)(2,1)}, u32[]{:S(2)}, u32[]{:S(2)}) async-start(bf16[512,4,768]{2,0,1:T(8,128)(2,1)} %bitcast.148), calls=%async_computation.1 | async-start | bytes 6291456 | tf_op jit(solution)/shard_map/all_to_all | solution.py:132
  346.0 108.3 %collective-permute-start = (bf16[512,3072]{1,0:T(8,128)(2,1)}, bf16[512,3072]{1,0:T(8,128)(2,1)}, u32[]{:S(2)}, u32[]{:S(2)}) collective-permute-start(bf16[512,3072]{1,0:T(8,128)(2,1)} %get-tuple-element.31), channel_id=1, source_target_pairs={{0,24},{8,0},{16,8},{24,16},{1,25},{9,1},{17,9},{25,17},{2,26},{10... | collective-permute-start | bytes 9437192 | tf_op jit(solution)/shard_map/ppermute | solution.py:25
  349.4 113.3 %collective-permute-start.2 = (bf16[512,3072]{1,0:T(8,128)(2,1)}, bf16[512,3072]{1,0:T(8,128)(2,1)}, u32[]{:S(2)}, u32[]{:S(2)}) collective-permute-start(bf16[512,3072]{1,0:T(8,128)(2,1)} %collective-permute-done.1), channel_id=1, source_target_pairs={{0,8},{8,16},{16,24},{24,0},{1,9},{9,17},{17,25},{25,1},{2,10},{10... | collective-permute-start | bytes 9437192 | tf_op jit(solution)/shard_map/ppermute | solution.py:23
  387.8 127.8 %all-to-all-start.2 = ((bf16[512,4,768]{2,0,1:T(8,128)(2,1)}), bf16[512,4,768]{2,0,1:T(8,128)(2,1)}, u32[]{:S(2)}, u32[]{:S(2)}) async-start(bf16[512,4,768]{2,0,1:T(8,128)(2,1)} %bitcast.147), calls=%async_computation.3 | async-start | bytes 6291456 | tf_op jit(solution)/shard_map/all_to_all | solution.py:134
  500.1 7.2 %copy-start.8 = (bf16[4,24,8,512]{3,2,0,1:T(8,128)(2,1)S(1)}, bf16[4,24,8,512]{3,2,0,1:T(8,128)(2,1)}, u32[]{:S(2)}) copy-start(bf16[4,24,8,512]{3,2,0,1:T(8,128)(2,1)} %copy.59) | copy-start | bytes 2359300
  515.5 15.7 %copy-start.4 = (f32[128,3072]{1,0:T(8,128)S(1)}, f32[128,3072]{1,0:T(8,128)}, u32[]{:S(2)}) copy-start(f32[128,3072]{1,0:T(8,128)} %reduce-scatter.2.cloned.1.call-done) | copy-start | bytes 4718596
Sparse Core Ops, SparseCore 0:
  24.6 190.0 all-reduce.4
  241.0 110.7 reduce-scatter.1
Sparse Core Ops, SparseCore 1:
  154.7 64.6 all-gather.2
  242.9 117.4 all-gather.4
